TPU v7x, 128 devices: a whole 4x4x4 slice. The times are simulated.
128 devices in a mesh: row: 8 (over y, core), col: 16 (over z, x).
Axes of the slice: x: 4, y: 4, z: 4, core: 2. Of those that a mesh axis runs over, the one named last changes fastest.
Arguments:
- rhs_scen: bfloat16 [1024, 131072], P(('row', 'col')), may hold values from -6 to 6
- factor_panels: bfloat16 [131072, 8192], P(('row', 'col')), as said below
Outputs:
- current: float32 [131072, 1024], P(('row', 'col'))
Inputs may be any that keep to these rules, and one draw needn't show every extreme that they name: `factor_panels`: in the rows of block b (b < 4, blocks of 2048 rows), every entry in the columns of later blocks is zero, and so is every entry above the diagonal of block b's own columns.
All inputs are finite; a program needn't handle non-finite values.
Results may differ from a plain program's by a relative error of at most 0.0023.
Values may be sent and summed in bfloat16 or wider, within the bound.
A program may use at most 128 MiB of HBM per device.

v0:
```python
import jax
import jax.numpy as jnp
from jax import lax
from jax.sharding import PartitionSpec as P

NB = 2048
STEPS = 4


def broadcast(value, axis, source):
    kept = jnp.where(lax.axis_index(axis) == source, value, 0).astype(value.dtype)
    return lax.psum(kept, axis)


def on_device(rhs_scen, factor_panels):
    rows_here = factor_panels.shape[0]
    per_block = NB // rows_here
    regrouped = lax.all_to_all(rhs_scen, ("row", "col"), split_axis=1, concat_axis=0, tiled=True)
    current = jnp.transpose(regrouped).astype(jnp.float32)
    my_block = lax.axis_index(("row", "col")) * rows_here // NB
    for block_step in range(STEPS):
        outgoing = current.astype(jnp.bfloat16)
        product = jnp.zeros(current.shape, jnp.float32)
        for member in range(per_block):
            received = broadcast(outgoing, ("row", "col"), block_step * per_block + member)
            first_col = block_step * NB + member * rows_here
            panel_cols = factor_panels[:, first_col : first_col + rows_here]
            product = product + jnp.dot(panel_cols, received, preferred_element_type=jnp.float32)
        current = jnp.where(my_block == block_step, product, current - product)
    return current


def solution(mesh):
    placed = (P(("row", "col"), None), P(("row", "col"), None))
    return jax.shard_map(
        on_device, mesh=mesh, in_specs=placed, out_specs=P(("row", "col"), None), check_vma=False
    )
```

profile of v0, /device:TPU:1, one launch (start us, length us, event | category | flops | bytes accessed | tf_op | source)
XLA Modules:
  0.0 720.6 jit_solution(16013752378215237109)
XLA Ops:
  6.5 11.5 %all-to-all-start = ((bf16[8,128,1024]{2,0,1:T(8,128)(2,1)}), bf16[8,128,1024]{2,0,1:T(8,128)(2,1)S(1)}, u32[]{:S(2)}, u32[]{:S(2)}) async-start(bf16[8,128,1024]{2,0,1:T(8,128)(2,1)} %bitcast.35), calls=%async_computation | async-start | bytes 4194304 | tf_op jit(solution)/shard_map/all_to_all | solution.py:18
  18.0 0.0 all-reduce.15.cloned.1.call-start
  18.1 29.4 %all-to-all-done = bf16[8,128,1024]{2,0,1:T(8,128)(2,1)S(1)} async-done(((bf16[8,128,1024]{2,0,1:T(8,128)(2,1)}), bf16[8,128,1024]{2,0,1:T(8,128)(2,1)S(1)}, u32[]{:S(2)}, u32[]{:S(2)}) %all-to-all-start) | async-done | bytes 2097184 | tf_op jit(solution)/shard_map/all_to_all | solution.py:18
  47.4 2.3 select_bitcast_fusion.1
  49.8 0.0 all-reduce.15.cloned.1.call-update
  49.8 0.0 all-reduce.13.cloned.1.call-start
  49.9 151.1 %all-reduce.15.cloned.1.call-done = (bf16[1024,1024]{0,1:T(8,128)(2,1)}, bf16[1024,1024]{0,1:T(8,128)(2,1)}) async-done(((bf16[1024,1024]{0,1:T(8,128)(2,1)}, bf16[1024,1024]{0,1:T(8,128)(2,1)}), (bf16[1024,1024]{0,1:T(8,128)(2,1)}, bf16[1024,1024]{0,1:T(8,128)(2,1)})) %all-reduce.15.cloned.1.call-update) | async-done | bytes 4194320 | tf_op jit(solution)/shard_map/psum | solution.py:12
  200.9 0.0 copy-start.5
  200.9 4.7 fusion.12
  205.7 0.0 copy-done.5
  205.7 7.8 %broadcast_select_fusion.3 = (bf16[1024,1024]{0,1:T(8,128)(2,1)}, bf16[1024,1024]{0,1:T(8,128)(2,1)}, f32[1024,1024]{0,1:T(8,128)}) fusion(pred[]{:T(512)S(6)} %eq.41, pred[]{:T(512)S(6)} %eq.45, bf16[8,128,1024]{2,0,1:T(8,128)(2,1)S(1)} %all-to-all-done, f32[1024,1024]{1,0:T(8,128)S(1)} %fusion.12, bf16[1024,1024]{0,1:T(8,128)(2,1)S(1)} %copy-done.5, ...), kind=kOutput, calls=%fused_computation.25 | convolution fusion | flops 2154823680 | bytes 18874372 | tf_op jit(solution)/shard_map/dot_general | solution.py:28
  213.5 0.0 all-reduce.13.cloned.1.call-update
  213.5 0.0 all-reduce.11.cloned.1.call-start
  213.6 153.0 %all-reduce.13.cloned.1.call-done = (bf16[1024,1024]{0,1:T(8,128)(2,1)}, bf16[1024,1024]{0,1:T(8,128)(2,1)}) async-done(((bf16[1024,1024]{0,1:T(8,128)(2,1)}, bf16[1024,1024]{0,1:T(8,128)(2,1)}), (bf16[1024,1024]{0,1:T(8,128)(2,1)}, bf16[1024,1024]{0,1:T(8,128)(2,1)})) %all-reduce.13.cloned.1.call-update) | async-done | bytes 4194320 | tf_op jit(solution)/shard_map/psum | solution.py:12
  366.6 4.7 fusion.8
  371.3 0.0 copy-done.1
  371.3 0.0 copy-done.4
  371.4 7.8 %broadcast_select_fusion.4 = (bf16[1024,1024]{0,1:T(8,128)(2,1)}, bf16[1024,1024]{0,1:T(8,128)(2,1)}, f32[1024,1024]{0,1:T(8,128)}) fusion(pred[]{:T(512)S(6)} %eq.39, pred[]{:T(512)S(6)} %eq.46, f32[1024,1024]{0,1:T(8,128)S(1)} %copy-done.1, f32[1024,1024]{1,0:T(8,128)S(1)} %fusion.8, bf16[1024,1024]{0,1:T(8,128)(2,1)S(1)} %copy-done.4, ...), kind=kOutput, calls=%fused_computation.26 | convolution fusion | flops 2153775104 | bytes 20971524 | tf_op jit(solution)/shard_map/dot_general | solution.py:28
  379.2 0.0 all-reduce.11.cloned.1.call-update
  379.2 0.2 all-reduce.9.cloned.1.call-start
  379.4 152.8 %all-reduce.11.cloned.1.call-done = (bf16[1024,1024]{0,1:T(8,128)(2,1)}, bf16[1024,1024]{0,1:T(8,128)(2,1)}) async-done(((bf16[1024,1024]{0,1:T(8,128)(2,1)}, bf16[1024,1024]{0,1:T(8,128)(2,1)}), (bf16[1024,1024]{0,1:T(8,128)(2,1)}, bf16[1024,1024]{0,1:T(8,128)(2,1)})) %all-reduce.11.cloned.1.call-update) | async-done | bytes 4194320 | tf_op jit(solution)/shard_map/psum | solution.py:12
  532.3 4.7 fusion.4
  537.0 0.0 copy-done
  537.0 0.0 copy-done.3
  537.0 7.8 %broadcast_select_fusion.5 = (bf16[1024,1024]{0,1:T(8,128)(2,1)}, bf16[1024,1024]{0,1:T(8,128)(2,1)}, f32[1024,1024]{0,1:T(8,128)}) fusion(pred[]{:T(512)S(6)} %eq.37, pred[]{:T(512)S(6)} %eq.47, f32[1024,1024]{0,1:T(8,128)S(1)} %copy-done, f32[1024,1024]{1,0:T(8,128)S(1)} %fusion.4, bf16[1024,1024]{0,1:T(8,128)(2,1)S(1)} %copy-done.3, ...), kind=kOutput, calls=%fused_computation.27 | convolution fusion | flops 2153775104 | bytes 20971524 | tf_op jit(solution)/shard_map/dot_general | solution.py:28
  544.9 0.0 all-reduce.9.cloned.1.call-update
  544.9 153.1 %all-reduce.9.cloned.1.call-done = (bf16[1024,1024]{0,1:T(8,128)(2,1)}, bf16[1024,1024]{0,1:T(8,128)(2,1)}) async-done(((bf16[1024,1024]{0,1:T(8,128)(2,1)}, bf16[1024,1024]{0,1:T(8,128)(2,1)}), (bf16[1024,1024]{0,1:T(8,128)(2,1)}, bf16[1024,1024]{0,1:T(8,128)(2,1)})) %all-reduce.9.cloned.1.call-update) | async-done | bytes 4194320 | tf_op jit(solution)/shard_map/psum | solution.py:12
  698.0 4.7 fusion
  702.8 0.0 copy-done.2
  702.8 0.0 copy-done.6
  702.8 6.0 subtract_select_fusion
  708.7 5.3 copy.3
  (6 shorter events, 0.0 us)
Async XLA Ops:
  6.5 40.9 %all-to-all-start = ((bf16[8,128,1024]{2,0,1:T(8,128)(2,1)}), bf16[8,128,1024]{2,0,1:T(8,128)(2,1)S(1)}, u32[]{:S(2)}, u32[]{:S(2)}) async-start(bf16[8,128,1024]{2,0,1:T(8,128)(2,1)} %bitcast.35), calls=%async_computation | async-start | bytes 4194304 | tf_op jit(solution)/shard_map/all_to_all | solution.py:18
  18.0 182.9 %all-reduce.15.cloned.1.call-start = ((), (), s32[]{:S(2)}) async-start(), calls=%async_computation.4 | async-start | bytes 8388608 | tf_op jit(solution)/shard_map/psum | solution.py:12
  49.8 316.8 %all-reduce.13.cloned.1.call-start = ((), (), s32[]{:S(2)}) async-start(), calls=%async_computation.3 | async-start | bytes 8388608 | tf_op jit(solution)/shard_map/psum | solution.py:12
  200.9 4.7 copy-start.5
  213.5 318.8 %all-reduce.11.cloned.1.call-start = ((), (), s32[]{:S(2)}) async-start(), calls=%async_computation.2 | async-start | bytes 8388608 | tf_op jit(solution)/shard_map/psum | solution.py:12
  366.6 4.7 copy-start.1
  366.6 4.8 copy-start.4
  379.2 318.8 %all-reduce.9.cloned.1.call-start = ((), (), s32[]{:S(2)}) async-start(), calls=%async_computation.1 | async-start | bytes 8388608 | tf_op jit(solution)/shard_map/psum | solution.py:12
  532.3 4.8 copy-start
  532.3 4.8 copy-start.3
  698.0 4.8 copy-start.2
  698.0 4.8 copy-start.6
Sparse Core Ops, SparseCore 0:
  49.9 150.9 all-reduce.14
  213.6 152.9 all-reduce.12
  379.3 152.9 all-reduce.10
  545.0 152.9 all-reduce.8
where the time goes:
time: 721 us
  waiting for transfers between devices  639 us (89%)
  matrix products  48.4 us (7%)
  between operations  13.3 us (2%)
  starting transfers between devices  11.8 us (2%)
    psum x4, waiting for transfers between devices, broadcast(): return lax.psum(kept, axis)  610 us
    dot_general x8, matrix products, on_device(): jnp.dot(panel_cols, received, preferred_element_type=jnp.float32)  48.4 us
    all_to_all x1, waiting for transfers between devices, on_device(): lax.all_to_all(rhs_scen, ('row', 'col'), split_axis=1, concat_axis=0, til...  29.4 us
  transfers between devices with their start and end apart: 5, of which 5 were waited for; matrix products, arithmetic and copies ran while one was open for 0% of the time, Pallas kernels for 0%

commit v1 on v0

v1 whole, which is shorter than its diff:
```python
import jax
import jax.numpy as jnp
from jax import lax
from jax.experimental import pallas as pl
from jax.experimental.pallas import tpu as pltpu
from jax.sharding import PartitionSpec as P

NB = 2048
STEPS = 4
ROWS = 1024
SCEN = 1024
T = 256
MESH = pl.DeviceIdType.MESH
ALL = slice(None)

COLOURS = (
    ("xzy", (0, ALL, pl.ds(0, 640)), (0, ALL, pl.ds(0, 384)), (0, ALL, pl.ds(384, 256))),
    ("yxz", (1, ALL, pl.ds(0, 640)), (1, ALL, pl.ds(0, 256)), (1, ALL, pl.ds(256, 384))),
    ("zyx", (ALL, ALL, pl.ds(640, 384)), (0, ALL, pl.ds(640, 384)), (1, ALL, pl.ds(640, 384))),
)
AXES = "yzx"


def kernel(rhs, panels, out, xs, acc, fac, rt, staged, own_sem, fac_sem, send_sem, recv_sem, xsend_sem, xrecv_sem,
           rt_send, rt_recv, sc_send):
    row, col = lax.axis_index("row"), lax.axis_index("col")
    me = row * 16 + col
    core = row % 2
    at = {"y": row // 2, "z": col // 4, "x": col % 4}
    my_block = me // 2

    def device(place, on_core):
        return (place["y"] * 2 + on_core, place["z"] * 4 + place["x"])

    def moved(axis, by):
        return {**at, axis: (at[axis] + by) % 4}

    def rows_to(dst):
        return rhs.at[:, pl.ds(pl.multiple_of(dst * ROWS, ROWS), ROWS)]

    def rt_copy(dst):
        return pltpu.make_async_remote_copy(
            src_ref=rows_to(dst), dst_ref=rt.at[core, at["y"], at["z"], at["x"]], send_sem=rt_send, recv_sem=rt_recv,
            device_id=(dst // 16, dst % 16), device_id_type=MESH)

    def rt_batch(first, last):
        def one(j, carry):
            dst = (me + j) % 128

            @pl.when((dst < 2) | (dst > 7))
            def _():
                rt_copy(dst).start()
            return carry
        lax.fori_loop(first, last, one, 0)

    def rt_wait():
        pltpu.make_async_copy(rt, rt, rt_recv).wait()

    def load_factor(k):
        cols = pl.ds(k * NB, NB)
        return pltpu.make_async_copy(panels.at[:, cols], fac.at[:, cols], fac_sem.at[k])

    def block_of(k, colour, fixed, part):
        return xs.at[(k, core) + tuple(fixed.get(a, ALL) for a in AXES) + part]

    def gather(k):
        started = []

        def ring(colour, phase, lane, by, centre, part):
            order = COLOURS[colour][0]
            axis, later = order[phase], order[phase + 1:]
            fixed = {a: at[a] for a in later}
            fixed[axis] = (at[axis] + centre) % 4
            block = block_of(k, colour, fixed, part)
            return pltpu.make_async_remote_copy(
                src_ref=block, dst_ref=block, send_sem=send_sem.at[phase, colour, lane],
                recv_sem=recv_sem.at[k, phase, colour, lane], device_id=device(moved(axis, by), core), device_id_type=MESH)

        def exchange(colour, step, centre):
            order, whole = COLOURS[colour][:2]
            axis = order[2]
            block = block_of(k, colour, {axis: (at[axis] + centre) % 4}, whole)
            copy = pltpu.make_async_remote_copy(
                src_ref=block, dst_ref=block, send_sem=xsend_sem.at[colour, step], recv_sem=xrecv_sem.at[k, colour, step],
                device_id=device(at, 1 - core), device_id_type=MESH)
            copy.start()
            started.append(copy)
            return copy

        swaps = []
        for phase in range(3):
            first = []
            for colour in range(3):
                whole = COLOURS[colour][1]
                first.append((ring(colour, phase, 0, 1, 0, whole), ring(colour, phase, 1, -1, 0, whole)))
            for pair in first:
                for copy in pair:
                    copy.start()
                    started.append(copy)
            if phase == 2:
                for colour in range(3):
                    swaps.append(exchange(colour, 0, 0))
            second = []
            for colour in range(3):
                _, _, low, high = COLOURS[colour]
                first[colour][0].wait_recv()
                onward = ring(colour, phase, 2, 1, -1, low)
                onward.start()
                first[colour][1].wait_recv()
                back = ring(colour, phase, 3, -1, 1, high)
                back.start()
                second += [onward, back]
            started += second
            if phase == 2:
                for colour in range(3):
                    swaps += [exchange(colour, 1, -1), exchange(colour, 2, 1)]
            for copy in second:
                copy.wait_recv()
        for colour in range(3):
            swaps.append(exchange(colour, 3, 2))
        for copy in swaps:
            copy.wait_recv()
        for copy in started:
            copy.wait_send()

    def product(k, m, n):
        rows = pl.ds(pl.multiple_of(m * T, T), T)
        cols = pl.ds(pl.multiple_of(n * T, T), T)
        left = fac[rows, pl.ds(pl.multiple_of(k * NB, NB), NB)]
        right = xs[k, :, :, :, :, :, :, cols].reshape(NB, T)
        return jnp.dot(left, right, preferred_element_type=jnp.float32)

    def turned(m, n):
        cols = pl.ds(pl.multiple_of(m * T, T), T)
        held = rt[n // 2, pl.ds((n % 2) * 2, 2), :, :, :, cols].reshape(T, T)
        eye = (lax.broadcasted_iota(jnp.int32, (T, T), 0) == lax.broadcasted_iota(jnp.int32, (T, T), 1))
        return lax.dot_general(eye.astype(jnp.bfloat16), held, (((1,), (1,)), ((), ())), preferred_element_type=jnp.float32)

    def tile(m, n):
        return pl.ds(pl.multiple_of(m * T, T), T), pl.ds(pl.multiple_of(n * T, T), T)

    def multiply_first():
        def one(i, carry):
            m, n = i % 4, i // 4
            rows, _ = tile(m, n)
            total = jnp.zeros((T, T), jnp.float32)
            for half in range(2):
                right = xs[0, n // 2, pl.ds((n % 2) * 2, 2), :, :, half].reshape(T, 1024)
                left = fac[rows, half * 1024:(half + 1) * 1024]
                total = total + lax.dot_general(left, right, (((1,), (1,)), ((), ())), preferred_element_type=jnp.float32)
            acc[tile(m, n)] = total
            return carry
        lax.fori_loop(0, 16, one, 0)

    def multiply(k):
        def one(i, carry):
            m, n = i % 4, i // 4
            kept = jnp.where(my_block == k, 0.0, acc[tile(m, n)])
            acc[tile(m, n)] = kept + product(k, m, n)
            return carry
        lax.fori_loop(0, 16, one, 0)

    def scatter_copies(k, m, i, go):
        z, x = i // 4, i % 4
        parity = me % 2
        src, dst = staged.at[m, z, x], xs.at[k, parity, m, z, x]
        here = (m == at["y"]) & (z == at["z"]) & (x == at["x"]) & (parity == core)

        @pl.when(here)
        def _():
            pltpu.make_async_copy(src, dst, own_sem.at[k]).start()

        @pl.when(jnp.logical_not(here))
        def _():
            pltpu.make_async_remote_copy(
                src_ref=src, dst_ref=dst, send_sem=sc_send, recv_sem=own_sem.at[k],
                device_id=(m * 2 + parity, i), device_id_type=MESH).start()

    def solve(k):
        rt_wait()

        def row_tile(m, carry):
            def col_tile(n, inner):
                solved = turned(m, n) - acc[tile(m, n)]
                staged[m, :, :, :, :, tile(m, n)[1]] = solved.astype(jnp.bfloat16).reshape(4, 4, 2, 8, T)
                return inner
            lax.fori_loop(0, 4, col_tile, 0)

            def send(i, inner):
                scatter_copies(k, m, i, True)
                return inner
            lax.fori_loop(0, 16, send, 0)
            return carry
        lax.fori_loop(0, 4, row_tile, 0)

    loads = [load_factor(k) for k in range(STEPS)]
    for load in loads:
        load.start()
    for half in range(2):
        pltpu.make_async_copy(
            rhs.at[:, half * 1024:(half + 1) * 1024], xs.at[0, core, at["y"], at["z"], at["x"], half], own_sem.at[0]).start()
    mine = pltpu.make_async_copy(rows_to(me), rt.at[core, at["y"], at["z"], at["x"]], rt_recv)
    mine.start()

    for owner in range(2, 8):
        @pl.when(me != owner)
        def _():
            rt_copy(jnp.int32(owner)).start()

    def own_piece(k):
        piece = xs.at[k, core, at["y"], at["z"], at["x"]]
        pltpu.make_async_copy(piece, piece, own_sem.at[k]).wait()

    own_piece(0)
    gather(0)
    for load in loads:
        load.wait()
    rt_batch(1, 44)
    multiply_first()

    def step(k, carry):
        @pl.when(my_block == k)
        def _():
            solve(k)
        own_piece(k)
        gather(k)

        @pl.when(k < STEPS - 1)
        def _():
            rt_batch(k * 43 + 1, jnp.minimum(k * 43 + 44, 128))
            multiply(k)
        return carry

    lax.fori_loop(1, STEPS, step, 0)

    is_owner = me < 2 * STEPS

    @pl.when((me < 2) | (me > 7))
    def _():
        rt_wait()

    for c in range(2):
        for pair in range(2):
            n = c * 2 + pair

            def last(m, carry):
                rows, _ = tile(m, n)
                kept = jnp.where(my_block == STEPS - 1, 0.0, acc[tile(m, n)])
                total = kept + product(STEPS - 1, m, n)
                value = jnp.where(is_owner, total, turned(m, n) - total)
                for y in range(2):
                    out[rows, ((pair * 2 + y) * 2 + c) * 128:((pair * 2 + y) * 2 + c + 1) * 128] = value[:, y * 128:(y + 1) * 128]
                return carry
            lax.fori_loop(0, 4, last, 0)

    pltpu.make_async_copy(rt.at[0], rt.at[0], rt_send).wait()
    pltpu.make_async_copy(rt.at[1, 0:3], rt.at[1, 0:3], rt_send).wait()
    pltpu.make_async_copy(rt.at[1, 3, 0:3], rt.at[1, 3, 0:3], rt_send).wait()
    pltpu.make_async_copy(rt.at[1, 3, 3, 0:3], rt.at[1, 3, 3, 0:3], rt_send).wait()

    @pl.when((me >= 2) & (me < 8))
    def _():
        @pl.when(me % 2 == 1)
        def _():
            pltpu.make_async_copy(staged, staged, sc_send).wait()

        @pl.when(me % 2 == 0)
        def _():
            pltpu.make_async_copy(staged.at[0:3], staged.at[0:3], sc_send).wait()
            pltpu.make_async_copy(staged.at[3, 0:3], staged.at[3, 0:3], sc_send).wait()
            pltpu.make_async_copy(staged.at[3, 3, 0:3], staged.at[3, 3, 0:3], sc_send).wait()


def on_device(rhs_scen, factor_panels):
    dma = pltpu.SemaphoreType.DMA
    return pl.pallas_call(
        kernel,
        out_shape=jax.ShapeDtypeStruct((ROWS, SCEN), jnp.float32),
        in_specs=[pl.BlockSpec(memory_space=pl.ANY)] * 2,
        out_specs=pl.BlockSpec(memory_space=pltpu.VMEM),
        scratch_shapes=[
            pltpu.VMEM((STEPS, 2, 4, 4, 4, 2, 8, 1024), jnp.bfloat16),
            pltpu.VMEM((ROWS, SCEN), jnp.float32),
            pltpu.VMEM((ROWS, STEPS * NB), jnp.bfloat16),
            pltpu.VMEM((2, 4, 4, 4, 8, ROWS), jnp.bfloat16),
            pltpu.VMEM((4, 4, 4, 2, 8, SCEN), jnp.bfloat16),
            dma((STEPS,)), dma((STEPS,)), dma((3, 3, 4)), dma((STEPS, 3, 3, 4)), dma((3, 4)), dma((STEPS, 3, 4)),
            dma, dma, dma,
        ],
        compiler_params=pltpu.CompilerParams(has_side_effects=True, vmem_limit_bytes=60 * 1024 * 1024),
        name="substitute",
    )(rhs_scen, factor_panels)


def solution(mesh):
    placed = (P(("row", "col"), None), P(("row", "col"), None))
    return jax.shard_map(
        on_device, mesh=mesh, in_specs=placed, out_specs=P(("row", "col"), None), check_vma=False
    )
```

time: 721 us -> 219 us (0.30)
  waiting for transfers between devices: 639 us -> 0 us
  Pallas kernels: 0 us -> 214 us
  matrix products: 48.4 us -> 0 us
  between operations: 13.3 us -> 0.01 us
  starting transfers between devices: 11.8 us -> 0 us
    psum x4 -> x0, waiting for transfers between devices: 610 us -> none  [broadcast(): return lax.psum(kept, axis)]
    pallas_call x0 -> x1, Pallas kernels: none -> 214 us  [on_device(): pl.pallas_call(kernel, out_shape=jax.ShapeDtypeStruct((ROWS, SCEN), jnp.f...]
    dot_general x8 -> x0, matrix products: 48.4 us -> none  [on_device(): jnp.dot(panel_cols, received, preferred_element_type=jnp.float32)]
    all_to_all x1 -> x0, waiting for transfers between devices: 29.4 us -> none  [on_device(): lax.all_to_all(rhs_scen, ('row', 'col'), split_axis=1, concat_axis=0, til...]
    all_to_all x1 -> x0, starting transfers between devices: 11.5 us -> none  [on_device(): lax.all_to_all(rhs_scen, ('row', 'col'), split_axis=1, concat_axis=0, til...]
  transfers between devices with their start and end apart: 5 -> 0, of which waited for: 5 -> 0; matrix products, arithmetic and copies ran while one was open for 0% -> 0% of each run, Pallas kernels for 0% -> 0%
where the time goes in v1:
time: 219 us; the launch traced here: 218 us
  Pallas kernels  214 us (98%)
  local copies, waits for them, and re-layouts  4.79 us (2%)
    pallas_call x1, Pallas kernels, on_device(): pl.pallas_call(kernel, out_shape=jax.ShapeDtypeStruct((ROWS, SCEN), jnp.f...  214 us
    unnamed x1, local copies, waits for them, and re-layouts  4.79 us

profile of v1, /device:TPU:1, one launch (start us, length us, event | category | flops | bytes accessed | tf_op | source)
XLA Modules:
  0.0 218.5 jit_solution(8628177991934650394)
XLA Ops:
  0.0 213.7 %substitute.1 = f32[1024,1024]{1,0:T(8,128)} custom-call(bf16[8,131072]{1,0:T(8,128)(2,1)} %rhs.1, bf16[1024,8192]{1,0:T(8,128)(2,1)} %panels.1), custom_call_target="tpu_custom_call" | custom-call | tf_op jit(solution)/shard_map/substitute/pallas_call | solution.py:276
  213.7 4.8 %copy.4 = f32[1024,1024]{1,0:T(8,128)} copy(f32[1024,1024]{1,0:T(8,128)} %substitute.1) | data formatting | bytes 8388608

commit v2 on v1

v2 whole, which is shorter than its diff:
```python
import jax
import jax.numpy as jnp
from jax import lax
from jax.experimental import pallas as pl
from jax.experimental.pallas import tpu as pltpu
from jax.sharding import PartitionSpec as P

NB = 2048
STEPS = 4
ROWS = 1024
SCEN = 1024
T = 256
MESH = pl.DeviceIdType.MESH
ALL = slice(None)

COLOURS = (
    ("xzy", (0, ALL, pl.ds(0, 640)), (0, ALL, pl.ds(0, 384)), (0, ALL, pl.ds(384, 256))),
    ("yxz", (1, ALL, pl.ds(0, 640)), (1, ALL, pl.ds(0, 256)), (1, ALL, pl.ds(256, 384))),
    ("zyx", (ALL, ALL, pl.ds(640, 384)), (0, ALL, pl.ds(640, 384)), (1, ALL, pl.ds(640, 384))),
)
AXES = "yzx"

WAYS = [(axis, by) for axis in "xyz" for by in (1, -1)]


def plan_relays():
    relays = {way: [[] for _ in range(4)] for way in WAYS}
    load = dict.fromkeys(WAYS, 0)
    for far in (1, 2, 3):
        for m in range(4):
            for dz in range(4):
                for dx in range(4):
                    offset = {"x": dx, "y": m, "z": dz}
                    moving = [a for a in "xyz" if offset[a]]
                    hops = sum(min(v, 4 - v) for v in offset.values())
                    if len(moving) != far or hops == 1:
                        continue
                    ways = [w for w in WAYS if offset[w[0]] == 2 or offset[w[0]] == w[1] % 4]
                    way = min(ways, key=lambda w: (load[w] + len(relays[w][m]), WAYS.index(w)))
                    load[way] += 1
                    relays[way][m].append((dz, dx))
    return relays


RELAYS = plan_relays()
MOST = max(len(part) for parts in RELAYS.values() for part in parts)


def kernel(rhs, panels, out, xs, acc, fac, rt, staged, passing, own_sem, fac_sem, send_sem, recv_sem, xsend_sem, xrecv_sem,
           rt_send, rt_recv, sc_send, pass_recv, pass_send):
    row, col = lax.axis_index("row"), lax.axis_index("col")
    me = row * 16 + col
    core = row % 2
    at = {"y": row // 2, "z": col // 4, "x": col % 4}
    my_block = me // 2

    def device(place, on_core):
        return (place["y"] * 2 + on_core, place["z"] * 4 + place["x"])

    def moved(axis, by):
        return {**at, axis: (at[axis] + by) % 4}

    def rows_to(dst):
        return rhs.at[:, pl.ds(pl.multiple_of(dst * ROWS, ROWS), ROWS)]

    def rt_copy(dst):
        return pltpu.make_async_remote_copy(
            src_ref=rows_to(dst), dst_ref=rt.at[core, at["y"], at["z"], at["x"]], send_sem=rt_send, recv_sem=rt_recv,
            device_id=(dst // 16, dst % 16), device_id_type=MESH)

    def rt_batch(first, last):
        def one(j, carry):
            dst = (me + j) % 128

            @pl.when((dst < 2) | (dst > 7))
            def _():
                rt_copy(dst).start()
            return carry
        lax.fori_loop(first, last, one, 0)

    def rt_wait():
        pltpu.make_async_copy(rt, rt, rt_recv).wait()

    def load_factor(k):
        cols = pl.ds(k * NB, NB)
        return pltpu.make_async_copy(panels.at[:, cols], fac.at[:, cols], fac_sem.at[k])

    def block_of(k, colour, fixed, part):
        return xs.at[(k, core) + tuple(fixed.get(a, ALL) for a in AXES) + part]

    def gather(k):
        started = []

        def ring(colour, phase, group, lane, by, centre, part):
            order = COLOURS[colour][0]
            axis, later = order[phase], order[phase + 1:]
            fixed = {a: at[a] for a in later}
            fixed[axis] = (at[axis] + centre) % 4
            slot = phase
            if phase == 2:
                fixed[order[1]] = (at[order[1]] + group) % 4
                slot = 2 + group % 4
            block = block_of(k, colour, fixed, part)
            copy = pltpu.make_async_remote_copy(
                src_ref=block, dst_ref=block, send_sem=send_sem.at[k, slot, colour, lane],
                recv_sem=recv_sem.at[k, slot, colour, lane], device_id=device(moved(axis, by), core), device_id_type=MESH)
            copy.start()
            started.append(copy)
            return copy

        def outward(colour, phase, group=0):
            whole = COLOURS[colour][1]
            return ring(colour, phase, group, 0, 1, 0, whole), ring(colour, phase, group, 1, -1, 0, whole)

        def onward(colour, phase, group=0):
            return ring(colour, phase, group, 2, 1, -1, COLOURS[colour][2])

        def back(colour, phase, group=0):
            return ring(colour, phase, group, 3, -1, 1, COLOURS[colour][3])

        def exchange(colour, step, centre):
            order, whole = COLOURS[colour][:2]
            axis = order[2]
            block = block_of(k, colour, {axis: (at[axis] + centre) % 4}, whole)
            copy = pltpu.make_async_remote_copy(
                src_ref=block, dst_ref=block, send_sem=xsend_sem.at[k, colour, step], recv_sem=xrecv_sem.at[k, colour, step],
                device_id=device(at, 1 - core), device_id_type=MESH)
            copy.start()
            started.append(copy)
            return copy

        three = range(3)
        first = [outward(c, 0) for c in three]
        far = []
        for c in three:
            first[c][0].wait_recv()
            one = onward(c, 0)
            first[c][1].wait_recv()
            far.append((one, back(c, 0)))
        second = []
        for c in three:
            far[c][0].wait_recv()
            far[c][1].wait_recv()
            second.append(outward(c, 1))
        last = {(c, 0): outward(c, 2, 0) for c in three}
        far = []
        for c in three:
            second[c][0].wait_recv()
            one = onward(c, 1)
            second[c][1].wait_recv()
            far.append((one, back(c, 1)))
        for group in (-1, 1):
            for c in three:
                last[c, group] = outward(c, 2, group)
        ends = []
        for c in three:
            last[c, 0][0].wait_recv()
            ends.append(onward(c, 2, 0))
            last[c, 0][1].wait_recv()
            ends.append(back(c, 2, 0))
        for c in three:
            far[c][0].wait_recv()
            far[c][1].wait_recv()
            last[c, 2] = outward(c, 2, 2)
        swaps = [exchange(c, 0, 0) for c in three]
        for group in (-1, 1, 2):
            for c in three:
                last[c, group][0].wait_recv()
                ends.append(onward(c, 2, group))
                last[c, group][1].wait_recv()
                ends.append(back(c, 2, group))
        for c in three:
            swaps += [exchange(c, 1, -1), exchange(c, 2, 1)]
        for copy in ends:
            copy.wait_recv()
        for c in three:
            swaps.append(exchange(c, 3, 2))
        for copy in swaps:
            copy.wait_recv()
        return started

    def rows_of(m):
        return pl.ds(pl.multiple_of(m * T, T), T)

    def product(k, m):
        return jnp.dot(fac[rows_of(m), k * NB:(k + 1) * NB], xs[k].reshape(NB, SCEN), preferred_element_type=jnp.float32)

    def first_product(m):
        total = None
        for half in range(2):
            right = xs[0, :, :, :, :, half].reshape(SCEN, 1024)
            left = fac[rows_of(m), half * 1024:(half + 1) * 1024]
            part = lax.dot_general(left, right, (((1,), (1,)), ((), ())), preferred_element_type=jnp.float32)
            total = part if total is None else total + part
        return total

    def turned(m):
        held = rt[:, :, :, :, :, rows_of(m)].reshape(SCEN, T)
        eye = (lax.broadcasted_iota(jnp.int32, (T, T), 0) == lax.broadcasted_iota(jnp.int32, (T, T), 1))
        return lax.dot_general(eye.astype(jnp.bfloat16), held, (((1,), (1,)), ((), ())), preferred_element_type=jnp.float32)

    def tiles(body):
        def one(m, carry):
            body(m)
            return carry
        lax.fori_loop(0, 4, one, 0)

    def multiply_first():
        def one(m):
            acc[rows_of(m), :] = first_product(m)
        tiles(one)

    def multiply(k):
        def one(m):
            kept = jnp.where(my_block == k, 0.0, acc[rows_of(m), :])
            acc[rows_of(m), :] = kept + product(k, m)
        tiles(one)

    def hand_out(k, m):
        parity = me % 2

        def send(dz, dx, target, place):
            pltpu.make_async_remote_copy(
                src_ref=staged.at[m, (at["z"] + dz) % 4, (at["x"] + dx) % 4], dst_ref=target, send_sem=sc_send,
                recv_sem=own_sem.at[k] if place is None else pass_recv.at[k, m],
                device_id=(m * 2 + parity, (at["z"] + dz) % 4 * 4 + (at["x"] + dx) % 4) if place is None
                else device(place, parity), device_id_type=MESH).start()

        most = max(len(RELAYS[way][m]) for way in WAYS)
        for i in range(most):
            for axis, by in WAYS:
                if i < len(RELAYS[axis, by][m]):
                    dz, dx = RELAYS[axis, by][m][i]
                    send(dz, dx, passing.at[k - 1, m, i], moved(axis, by))
        for dz in range(4):
            for dx in range(4):
                hops = sum(min(v, 4 - v) for v in (dz, dx, m))
                if hops > 1:
                    continue
                z, x = (at["z"] + dz) % 4, (at["x"] + dx) % 4
                target = xs.at[k, parity, m, z, x]
                if hops == 1:
                    send(dz, dx, target, None)
                else:
                    @pl.when(parity == 0)
                    def _():
                        pltpu.make_async_copy(staged.at[m, z, x], target, own_sem.at[k]).start()

                    @pl.when(parity == 1)
                    def _():
                        send(dz, dx, target, None)

    def solve(k, total, ready):
        for m in range(4):
            if ready:
                solved = turned(m) - total(m)
            else:
                solved = turned(m) - acc[rows_of(m), :]
            staged[m] = solved.astype(jnp.bfloat16).reshape(4, 4, 2, 8, SCEN)
            hand_out(k, m)

    def roles(k):
        dx = (at["x"] - (2 * k) % 4 - core) % 4
        dz = (at["z"] - k // 2) % 4
        offset = {"x": dx, "y": at["y"], "z": dz}
        for axis, by in WAYS:
            here = offset[axis] == by % 4
            for other in "xyz":
                if other != axis:
                    here = here & (offset[other] == 0)
            yield (axis, by), here

    def pass_on(k):
        for (axis, by), here in roles(k):
            @pl.when(here)
            def _():
                for m in range(4):
                    held = RELAYS[axis, by][m]
                    if not held:
                        continue
                    got = passing.at[k - 1, m, 0:len(held)]
                    pltpu.make_async_copy(got, got, pass_recv.at[k, m]).wait()
                    for i, (dz, dx) in enumerate(held):
                        z, x = (k // 2 + dz) % 4, ((2 * k) % 4 + core + dx) % 4
                        pltpu.make_async_remote_copy(
                            src_ref=passing.at[k - 1, m, i], dst_ref=xs.at[k, core, m, z, x], send_sem=pass_send.at[k],
                            recv_sem=own_sem.at[k], device_id=(m * 2 + core, z * 4 + x), device_id_type=MESH).start()

    def pass_done(k):
        for way, here in roles(k):
            @pl.when(here)
            def _():
                for m in range(4):
                    if RELAYS[way][m]:
                        got = passing.at[k - 1, m, 0:len(RELAYS[way][m])]
                        pltpu.make_async_copy(got, got, pass_send.at[k]).wait()

    loads = [load_factor(k) for k in range(STEPS)]
    for half in range(2):
        pltpu.make_async_copy(
            rhs.at[:, half * 1024:(half + 1) * 1024], xs.at[0, core, at["y"], at["z"], at["x"], half], own_sem.at[0]).start()
    mine = pltpu.make_async_copy(rows_to(me), rt.at[core, at["y"], at["z"], at["x"]], rt_recv)
    mine.start()

    for load in loads:
        load.start()

    barrier = pltpu.get_barrier_semaphore()
    for axis, by in WAYS:
        pl.semaphore_signal(barrier, inc=1, device_id=device(moved(axis, by), core), device_id_type=MESH)
    pl.semaphore_signal(barrier, inc=1, device_id=device(at, 1 - core), device_id_type=MESH)
    pl.semaphore_wait(barrier, 7)

    def own_piece(k):
        piece = xs.at[k, core, at["y"], at["z"], at["x"]]
        pltpu.make_async_copy(piece, piece, own_sem.at[k]).wait()

    own_piece(0)
    started = gather(0)
    for load in loads:
        load.wait()

    for owner in range(2, 8):
        @pl.when(me != owner)
        def _():
            rt_copy(jnp.int32(owner)).start()

    rt_batch(1, 36)

    @pl.when(my_block == 1)
    def _():
        multiply_first()
        rt_wait()
        solve(1, None, False)

    @pl.when(my_block != 1)
    def _():
        multiply_first()

    pass_on(1)
    own_piece(1)
    started += gather(1)
    for k in (2, 3):
        rt_batch(*{2: (36, 82), 3: (82, 128)}[k])

        @pl.when(my_block == k)
        def _():
            rt_wait()
            solve(k, lambda m: acc[rows_of(m), :] + product(k - 1, m), True)

        @pl.when(my_block != k)
        def _():
            multiply(k - 1)

        pass_on(k)
        own_piece(k)
        started += gather(k)

    is_owner = me < 2 * STEPS

    @pl.when((me < 2) | (me > 7))
    def _():
        rt_wait()

    def last(m):
        kept = jnp.where(my_block == STEPS - 1, 0.0, acc[rows_of(m), :])
        total = kept + product(STEPS - 1, m)
        value = jnp.where(is_owner, total, turned(m) - total)
        for c in range(2):
            for y in range(4):
                held = c * 4 + y
                out[rows_of(m), (y * 2 + c) * 128:(y * 2 + c + 1) * 128] = value[:, held * 128:(held + 1) * 128]
    tiles(last)

    for copy in started:
        copy.wait_send()
    pltpu.make_async_copy(rt.at[0], rt.at[0], rt_send).wait()
    pltpu.make_async_copy(rt.at[1, 0:3], rt.at[1, 0:3], rt_send).wait()
    pltpu.make_async_copy(rt.at[1, 3, 0:3], rt.at[1, 3, 0:3], rt_send).wait()
    pltpu.make_async_copy(rt.at[1, 3, 3, 0:3], rt.at[1, 3, 3, 0:3], rt_send).wait()

    @pl.when((me >= 2) & (me < 8))
    def _():
        @pl.when(me % 2 == 1)
        def _():
            pltpu.make_async_copy(staged, staged, sc_send).wait()

        @pl.when(me % 2 == 0)
        def _():
            pltpu.make_async_copy(staged.at[0:3], staged.at[0:3], sc_send).wait()
            pltpu.make_async_copy(staged.at[3, 0:3], staged.at[3, 0:3], sc_send).wait()
            pltpu.make_async_copy(staged.at[3, 3, 0:3], staged.at[3, 3, 0:3], sc_send).wait()


    for k in (1, 2, 3):
        pass_done(k)


def on_device(rhs_scen, factor_panels):
    dma = pltpu.SemaphoreType.DMA
    return pl.pallas_call(
        kernel,
        out_shape=pltpu.VMEM((ROWS, SCEN), jnp.float32),
        in_specs=[pl.BlockSpec(memory_space=pl.ANY)] * 2,
        out_specs=pl.BlockSpec(memory_space=pltpu.VMEM),
        scratch_shapes=[
            pltpu.VMEM((STEPS, 2, 4, 4, 4, 2, 8, 1024), jnp.bfloat16),
            pltpu.VMEM((ROWS, SCEN), jnp.float32),
            pltpu.VMEM((ROWS, STEPS * NB), jnp.bfloat16),
            pltpu.VMEM((2, 4, 4, 4, 8, ROWS), jnp.bfloat16),
            pltpu.VMEM((4, 4, 4, 2, 8, SCEN), jnp.bfloat16),
            pltpu.VMEM((STEPS - 1, 4, MOST, 2, 8, SCEN), jnp.bfloat16),
            dma((STEPS,)), dma((STEPS,)), dma((STEPS, 6, 3, 4)), dma((STEPS, 6, 3, 4)), dma((STEPS, 3, 4)), dma((STEPS, 3, 4)),
            dma, dma, dma, dma((STEPS, 4)), dma((STEPS,)),
        ],
        compiler_params=pltpu.CompilerParams(collective_id=0, has_side_effects=True, vmem_limit_bytes=52 * 1024 * 1024),
        name="substitute",
    )(rhs_scen, factor_panels)


def solution(mesh):
    placed = (P(("row", "col"), None), P(("row", "col"), None))
    return jax.shard_map(
        on_device, mesh=mesh, in_specs=placed, out_specs=P(("row", "col"), None), check_vma=False
    )
```

time: 219 us -> 188 us (0.86)
  Pallas kernels: 214 us -> 186 us
  local copies, waits for them, and re-layouts: 4.79 us -> 2.02 us
    pallas_call x1, Pallas kernels: 214 us -> 186 us  [on_device(): pl.pallas_call(kernel, out_shape=pltpu.VMEM((ROWS, SCEN), jnp.float32), i...]
    unnamed x1, local copies, waits for them, and re-layouts: 4.79 us -> 2.02 us
where the time goes in v2:
time: 188 us
  Pallas kernels  186 us (99%)
  local copies, waits for them, and re-layouts  2.02 us (1%)
    pallas_call x1, Pallas kernels, on_device(): pl.pallas_call(kernel, out_shape=pltpu.VMEM((ROWS, SCEN), jnp.float32), i...  186 us

profile of v2, /device:TPU:1, one launch (start us, length us, event | category | flops | bytes accessed | tf_op | source)
XLA Modules:
  0.0 187.7 jit_solution(11851238654111128084)
XLA Ops:
  0.0 185.7 %substitute.1 = f32[1024,1024]{1,0:T(8,128)S(1)} custom-call(bf16[8,131072]{1,0:T(8,128)(2,1)} %rhs.1, bf16[1024,8192]{1,0:T(8,128)(2,1)} %panels.1), custom_call_target="tpu_custom_call" | custom-call | tf_op jit(solution)/shard_map/substitute/pallas_call | solution.py:401
  185.7 2.0 %copy.4 = f32[1024,1024]{1,0:T(8,128)} copy(f32[1024,1024]{1,0:T(8,128)S(1)} %substitute.1) | data formatting | bytes 8388608

commit v3 on v2

v3 whole, which is shorter than its diff:
```python
import jax
import jax.numpy as jnp
from jax import lax
from jax.experimental import pallas as pl
from jax.experimental.pallas import tpu as pltpu
from jax.sharding import PartitionSpec as P

NB = 2048
STEPS = 4
ROWS = 1024
SCEN = 1024
T = 256
MESH = pl.DeviceIdType.MESH
ALL = slice(None)

COLOURS = (
    ("xzy", (0, ALL, pl.ds(0, 640)), (0, ALL, pl.ds(0, 384)), (0, ALL, pl.ds(384, 256))),
    ("yxz", (1, ALL, pl.ds(0, 640)), (1, ALL, pl.ds(0, 256)), (1, ALL, pl.ds(256, 384))),
    ("zyx", (ALL, ALL, pl.ds(640, 384)), (0, ALL, pl.ds(640, 384)), (1, ALL, pl.ds(640, 384))),
)
ORDER = (2, 1, 3, 0)
AXES = "yzx"

WAYS = [(axis, by) for axis in "xyz" for by in (1, -1)]


def plan_relays():
    relays = {way: [[] for _ in range(4)] for way in WAYS}
    load = dict.fromkeys(WAYS, 0)
    for far in (1, 2, 3):
        for m in range(4):
            for dz in range(4):
                for dx in range(4):
                    offset = {"x": dx, "y": m, "z": dz}
                    moving = [a for a in "xyz" if offset[a]]
                    hops = sum(min(v, 4 - v) for v in offset.values())
                    if len(moving) != far or hops == 1:
                        continue
                    ways = [w for w in WAYS if offset[w[0]] == 2 or offset[w[0]] == w[1] % 4]
                    way = min(ways, key=lambda w: (load[w] + len(relays[w][m]), WAYS.index(w)))
                    load[way] += 1
                    relays[way][m].append((dz, dx))
    return relays


RELAYS = plan_relays()
MOST = max(len(part) for parts in RELAYS.values() for part in parts)
TOTAL = max(sum(len(part) for part in parts) for parts in RELAYS.values())


def kernel(rhs, panels, out, xs, acc, fac, rt, staged, passing, feeding, own_sem, fac_sem, send_sem, near_sem, last_sem,
           far_sem, swap_sem, rt_send, rt_recv, sc_send, pass_recv, pass_send,
           feed_recv, feed_send):
    row, col = lax.axis_index("row"), lax.axis_index("col")
    me = row * 16 + col
    core = row % 2
    at = {"y": row // 2, "z": col // 4, "x": col % 4}
    my_block = me // 2

    def device(place, on_core):
        return (place["y"] * 2 + on_core, place["z"] * 4 + place["x"])

    def moved(axis, by):
        return {**at, axis: (at[axis] + by) % 4}

    def rows_to(dst):
        return rhs.at[:, pl.ds(pl.multiple_of(dst * ROWS, ROWS), ROWS)]

    def rt_copy(dst):
        return pltpu.make_async_remote_copy(
            src_ref=rows_to(dst), dst_ref=rt.at[core, at["y"], at["z"], at["x"]], send_sem=rt_send, recv_sem=rt_recv,
            device_id=(dst // 16, dst % 16), device_id_type=MESH)

    def rt_batch(first, last):
        def one(j, carry):
            dst = (me + j) % 128

            @pl.when((dst < 2) | (dst > 7))
            def _():
                rt_copy(dst).start()
            return carry
        lax.fori_loop(first, last, one, 0)

    def rt_wait():
        pltpu.make_async_copy(rt, rt, rt_recv).wait()

    def feeds():
        for h in range(2):
            dx = (at["x"] - 2 - h) % 4
            yield h, {"x": dx, "y": at["y"], "z": at["z"]}

    def away(offset):
        apart = [jnp.minimum(offset[a], 4 - offset[a]) for a in "xyz"]
        return apart[0] + apart[1] + apart[2]

    def listed(way):
        return [(dz, m, dx) for m in range(4) for dz, dx in RELAYS[way][m]]

    def feed():
        for h, offset in feeds():
            hops = away(offset)

            @pl.when((hops < 2) & (me != 2 + h))
            def _():
                rt_copy(jnp.int32(2 + h)).start()
            for way in WAYS:
                axis, by = way
                relay = {"x": 2 + h, "y": 0, "z": 0}
                relay[axis] = (relay[axis] + by) % 4
                for i, (dz, dy, dx) in enumerate(listed(way)):
                    @pl.when((offset["x"] == dx) & (offset["y"] == dy) & (offset["z"] == dz))
                    def _():
                        pltpu.make_async_remote_copy(
                            src_ref=rows_to(jnp.int32(2 + h)), dst_ref=feeding.at[i], send_sem=rt_send, recv_sem=feed_recv,
                            device_id=device(relay, core), device_id_type=MESH).start()

    def feed_roles():
        for h, offset in feeds():
            for axis, by in WAYS:
                here = offset[axis] == by % 4
                for other in "xyz":
                    if other != axis:
                        here = here & (offset[other] == 0)
                yield h, (axis, by), here

    def feed_on():
        for h, way, here in feed_roles():
            @pl.when(here)
            def _():
                held = listed(way)
                got = feeding.at[0:len(held)]
                pltpu.make_async_copy(got, got, feed_recv).wait()
                for i, (dz, dy, dx) in enumerate(held):
                    pltpu.make_async_remote_copy(
                        src_ref=feeding.at[i], dst_ref=rt.at[core, dy, dz, (2 + h + dx) % 4], send_sem=feed_send,
                        recv_sem=rt_recv, device_id=(0, 2 + h), device_id_type=MESH).start()

    def feed_done():
        for h, way, here in feed_roles():
            @pl.when(here)
            def _():
                got = feeding.at[0:len(listed(way))]
                pltpu.make_async_copy(got, got, feed_send).wait()

    def load_factor(k):
        cols = pl.ds(k * NB, NB)
        return pltpu.make_async_copy(panels.at[:, cols], fac.at[:, cols], fac_sem.at[k])

    def block_of(k, colour, fixed, part):
        return xs.at[(k, core) + tuple(fixed.get(a, ALL) for a in AXES) + part]

    def gather(k, between, first_half):
        turn = k % 2

        def send(block, sem, device_id):
            copy = pltpu.make_async_remote_copy(
                src_ref=block, dst_ref=block, send_sem=send_sem, recv_sem=sem, device_id=device_id, device_id_type=MESH)
            copy.start()
            return copy

        def ring(colour, phase, group, sem, by, centre, part):
            order = COLOURS[colour][0]
            axis, later = order[phase], order[phase + 1:]
            fixed = {a: at[a] for a in later}
            fixed[axis] = (at[axis] + centre) % 4
            if phase == 2:
                fixed[order[1]] = (at[order[1]] + group) % 4
            return send(block_of(k, colour, fixed, part), sem, device(moved(axis, by), core))

        def outward(colour, phase):
            whole = COLOURS[colour][1]
            return [ring(colour, phase, 0, near_sem.at[turn, phase, colour, lane], by, 0, whole)
                    for lane, by in enumerate((1, -1, 2))]

        def outward_last(colour, group):
            whole = COLOURS[colour][1]
            return [ring(colour, 2, group, last_sem.at[turn, group % 4, colour, lane], by, 0, whole)
                    for lane, by in enumerate((1, -1))]

        def forward(colour, group, copies):
            _, _, low, high = COLOURS[colour]
            copies[0].wait_recv()
            ring(colour, 2, group, far_sem.at[turn], 1, -1, low)
            copies[1].wait_recv()
            ring(colour, 2, group, far_sem.at[turn], -1, 1, high)

        def exchange(colour, centre):
            order, whole = COLOURS[colour][:2]
            axis = order[2]
            send(block_of(k, colour, {axis: (at[axis] + centre) % 4}, whole), swap_sem.at[turn], device(at, 1 - core))

        three = range(3)
        first = [outward(c, 0) for c in three]
        second = []
        for c in three:
            for copy in first[c]:
                copy.wait_recv()
            second.append(outward(c, 1))
        last = {(c, 0): outward_last(c, 0) for c in three}
        between[0]()
        for lane, group in enumerate((-1, 1, 2)):
            for c in three:
                second[c][lane].wait_recv()
                last[c, group] = outward_last(c, group)
        between[1]()
        for c in three:
            exchange(c, 0)
        for group in (0, -1, 1, 2):
            for c in three:
                forward(c, group, last[c, group])
        between[2]()
        for c in three:
            exchange(c, -1)
            exchange(c, 1)
        plane = xs.at[k, core, 0]
        other = xs.at[k, 1 - core]

        def own_half():
            pltpu.make_async_copy(plane, plane, far_sem.at[turn]).wait()
            for c in three:
                exchange(c, 2)

        def other_half():
            pltpu.make_async_copy(other, other, swap_sem.at[turn]).wait()

        @pl.when(core == 1)
        def _():
            own_half()

        @pl.when(core == 0)
        def _():
            other_half()
        first_half()

        @pl.when(core == 1)
        def _():
            other_half()

        @pl.when(core == 0)
        def _():
            own_half()

    def gathers_sent():
        for k in range(STEPS):
            for part in (xs.at[k, 0], xs.at[k, 1, 0:3], xs.at[k, 1, 3, 0:3], xs.at[k, 1, 3, 3, 0:3]):
                pltpu.make_async_copy(part, part, send_sem).wait()

    def rows_of(m):
        return pl.ds(pl.multiple_of(m * T, T), T)

    def product(k, half, m):
        cols = pl.ds(k * NB + half * 1024, 1024)
        return jnp.dot(fac[rows_of(m), cols], xs[k, half].reshape(1024, SCEN), preferred_element_type=jnp.float32)

    def first_product(half, m):
        total = None
        for part in range(2):
            right = xs[0, half, :, :, :, part].reshape(SCEN // 2, 1024)
            left = fac[rows_of(m), part * 1024:(part + 1) * 1024]
            more = lax.dot_general(left, right, (((1,), (1,)), ((), ())), preferred_element_type=jnp.float32)
            total = more if total is None else total + more
        return total

    def turned(m):
        held = rt[:, :, :, :, :, rows_of(m)].reshape(SCEN, T)
        eye = (lax.broadcasted_iota(jnp.int32, (T, T), 0) == lax.broadcasted_iota(jnp.int32, (T, T), 1))
        return lax.dot_general(eye.astype(jnp.bfloat16), held, (((1,), (1,)), ((), ())), preferred_element_type=jnp.float32)

    def tiles(body):
        def one(m, carry):
            body(m)
            return carry
        lax.fori_loop(0, 4, one, 0)

    def multiply(k, half):
        def one(m):
            if k == 0:
                acc[rows_of(m), half * 512:(half + 1) * 512] = first_product(half, m)
            elif half == 1:
                kept = jnp.where(my_block == k, 0.0, acc[rows_of(m), :])
                acc[rows_of(m), :] = kept + product(k, 1, m)
            else:
                acc[rows_of(m), :] += product(k, 0, m)
        tiles(one)

    def hand_out(k, m):
        parity = me % 2

        def send(dz, dx, target, place):
            pltpu.make_async_remote_copy(
                src_ref=staged.at[m, (at["z"] + dz) % 4, (at["x"] + dx) % 4], dst_ref=target, send_sem=sc_send,
                recv_sem=own_sem.at[k] if place is None else pass_recv.at[k - 1, m],
                device_id=(m * 2 + parity, (at["z"] + dz) % 4 * 4 + (at["x"] + dx) % 4) if place is None
                else device(place, parity), device_id_type=MESH).start()

        most = max(len(RELAYS[way][m]) for way in WAYS)
        for i in range(most):
            for axis, by in WAYS:
                if i < len(RELAYS[axis, by][m]):
                    dz, dx = RELAYS[axis, by][m][i]
                    send(dz, dx, passing.at[k - 1, m, i], moved(axis, by))
        for dz in range(4):
            for dx in range(4):
                hops = sum(min(v, 4 - v) for v in (dz, dx, m))
                if hops > 1:
                    continue
                z, x = (at["z"] + dz) % 4, (at["x"] + dx) % 4
                target = xs.at[k, parity, m, z, x]
                if hops == 1:
                    send(dz, dx, target, None)
                else:
                    @pl.when(parity == 0)
                    def _():
                        pltpu.make_async_copy(staged.at[m, z, x], target, own_sem.at[k]).start()

                    @pl.when(parity == 1)
                    def _():
                        send(dz, dx, target, None)

    def solve(k):
        for m in ORDER:
            wanted = turned(m)
            if k == 1:
                solved = wanted - jnp.concatenate([first_product(0, m), acc[rows_of(m), 512:]], axis=1)
            else:
                solved = wanted - (acc[rows_of(m), :] + product(k - 1, 0, m))
            staged[m] = solved.astype(jnp.bfloat16).reshape(4, 4, 2, 8, SCEN)
            hand_out(k, m)

    def roles(k):
        dx = (at["x"] - (2 * k) % 4 - core) % 4
        dz = (at["z"] - k // 2) % 4
        offset = {"x": dx, "y": at["y"], "z": dz}
        for axis, by in WAYS:
            here = offset[axis] == by % 4
            for other in "xyz":
                if other != axis:
                    here = here & (offset[other] == 0)
            yield (axis, by), here

    def pass_on(k):
        for (axis, by), here in roles(k):
            @pl.when(here)
            def _():
                for m in ORDER:
                    held = RELAYS[axis, by][m]
                    if not held:
                        continue
                    got = passing.at[k - 1, m, 0:len(held)]
                    pltpu.make_async_copy(got, got, pass_recv.at[k - 1, m]).wait()
                    for i, (dz, dx) in enumerate(held):
                        z, x = (k // 2 + dz) % 4, ((2 * k) % 4 + core + dx) % 4
                        pltpu.make_async_remote_copy(
                            src_ref=passing.at[k - 1, m, i], dst_ref=xs.at[k, core, m, z, x], send_sem=pass_send,
                            recv_sem=own_sem.at[k], device_id=(m * 2 + core, z * 4 + x), device_id_type=MESH).start()

    def pass_done(k):
        for way, here in roles(k):
            @pl.when(here)
            def _():
                for m in range(4):
                    if RELAYS[way][m]:
                        got = passing.at[k - 1, m, 0:len(RELAYS[way][m])]
                        pltpu.make_async_copy(got, got, pass_send).wait()

    loads = [load_factor(k) for k in range(STEPS)]
    for half in range(2):
        pltpu.make_async_copy(
            rhs.at[:, half * 1024:(half + 1) * 1024], xs.at[0, core, at["y"], at["z"], at["x"], half], own_sem.at[0]).start()
    mine = pltpu.make_async_copy(rows_to(me), rt.at[core, at["y"], at["z"], at["x"]], rt_recv)
    mine.start()

    for load in loads:
        load.start()

    barrier = pltpu.get_barrier_semaphore()
    for axis in AXES:
        for by in (1, 2, 3):
            pl.semaphore_signal(barrier, inc=1, device_id=device(moved(axis, by), core), device_id_type=MESH)
    pl.semaphore_signal(barrier, inc=1, device_id=device(at, 1 - core), device_id_type=MESH)

    expected = 10
    for h, offset in feeds():
        hops = away(offset)
        expected = expected + ((hops > 1) | ((hops == 1) & (core == 1))).astype(jnp.int32)

        @pl.when(me == 2 + h)
        def _():
            for axis, by in WAYS:
                pl.semaphore_signal(barrier, inc=1, device_id=device(moved(axis, by), 1), device_id_type=MESH)
    for h, way, here in feed_roles():
        @pl.when(here)
        def _():
            for dz, dy, dx in listed(way):
                place = {"y": dy, "z": dz, "x": (2 + h + dx) % 4}
                pl.semaphore_signal(barrier, inc=1, device_id=device(place, core), device_id_type=MESH)
    pl.semaphore_wait(barrier, expected)

    def own_piece(k):
        piece = xs.at[k, core, at["y"], at["z"], at["x"]]
        pltpu.make_async_copy(piece, piece, own_sem.at[k]).wait()

    def to_owners(*owners):
        for owner in owners:
            @pl.when(me != owner)
            def _():
                rt_copy(jnp.int32(owner)).start()

    def batch(first, last):
        return lambda: rt_batch(first, last)

    def nothing():
        pass

    own_piece(0)
    def load_wait():
        for load in loads:
            load.wait()

    def half_of(k):
        return lambda: multiply(k, 1)

    def first_half():
        load_wait()
        multiply(0, 1)

    slots = [(1, 1, 1, 13), (13, 19, 25, 55), (55, 59, 63, 91), (91, 99, 107, 128)]

    def after_first():
        to_owners(4, 5, 6, 7)
        rt_batch(slots[0][2], slots[0][3])

    gather(0, (feed, nothing, feed_on), first_half)
    after_first()
    for k in (1, 2, 3):
        @pl.when(my_block == k)
        def _():
            rt_wait()
            solve(k)

        @pl.when(my_block != k)
        def _():
            multiply(k - 1, 0)

        pass_on(k)
        own_piece(k)
        cuts = slots[k]
        gather(k, [batch(cuts[i], cuts[i + 1]) for i in range(3)], half_of(k))

    is_owner = me < 2 * STEPS

    @pl.when((me < 2) | (me > 7))
    def _():
        rt_wait()

    def last(m):
        total = acc[rows_of(m), :] + product(STEPS - 1, 0, m)
        value = jnp.where(is_owner, total, turned(m) - total)
        for c in range(2):
            for y in range(4):
                held = c * 4 + y
                out[rows_of(m), (y * 2 + c) * 128:(y * 2 + c + 1) * 128] = value[:, held * 128:(held + 1) * 128]
    tiles(last)

    gathers_sent()
    pltpu.make_async_copy(rt.at[0], rt.at[0], rt_send).wait()
    pltpu.make_async_copy(rt.at[1, 0:3], rt.at[1, 0:3], rt_send).wait()
    pltpu.make_async_copy(rt.at[1, 3, 0:3], rt.at[1, 3, 0:3], rt_send).wait()
    pltpu.make_async_copy(rt.at[1, 3, 3, 0:3], rt.at[1, 3, 3, 0:3], rt_send).wait()

    @pl.when((me >= 2) & (me < 8))
    def _():
        @pl.when(me % 2 == 1)
        def _():
            pltpu.make_async_copy(staged, staged, sc_send).wait()

        @pl.when(me % 2 == 0)
        def _():
            pltpu.make_async_copy(staged.at[0:3], staged.at[0:3], sc_send).wait()
            pltpu.make_async_copy(staged.at[3, 0:3], staged.at[3, 0:3], sc_send).wait()
            pltpu.make_async_copy(staged.at[3, 3, 0:3], staged.at[3, 3, 0:3], sc_send).wait()


    for k in (1, 2, 3):
        pass_done(k)
    feed_done()


def on_device(rhs_scen, factor_panels):
    dma = pltpu.SemaphoreType.DMA
    return pl.pallas_call(
        kernel,
        out_shape=pltpu.VMEM((ROWS, SCEN), jnp.float32),
        in_specs=[pl.BlockSpec(memory_space=pl.ANY)] * 2,
        out_specs=pl.BlockSpec(memory_space=pltpu.VMEM),
        scratch_shapes=[
            pltpu.VMEM((STEPS, 2, 4, 4, 4, 2, 8, 1024), jnp.bfloat16),
            pltpu.VMEM((ROWS, SCEN), jnp.float32),
            pltpu.VMEM((ROWS, STEPS * NB), jnp.bfloat16),
            pltpu.VMEM((2, 4, 4, 4, 8, ROWS), jnp.bfloat16),
            pltpu.VMEM((4, 4, 4, 2, 8, SCEN), jnp.bfloat16),
            pltpu.VMEM((STEPS - 1, 4, MOST, 2, 8, SCEN), jnp.bfloat16),
            pltpu.VMEM((TOTAL, 8, ROWS), jnp.bfloat16),
            dma((STEPS,)), dma((STEPS,)), dma, dma((2, 2, 3, 3)), dma((2, 4, 3, 2)), dma((2,)), dma((2,)),
            dma, dma, dma, dma((STEPS - 1, 4)), dma, dma, dma,
        ],
        compiler_params=pltpu.CompilerParams(collective_id=0, has_side_effects=True, vmem_limit_bytes=52 * 1024 * 1024),
        name="substitute",
    )(rhs_scen, factor_panels)


def solution(mesh):
    placed = (P(("row", "col"), None), P(("row", "col"), None))
    return jax.shard_map(
        on_device, mesh=mesh, in_specs=placed, out_specs=P(("row", "col"), None), check_vma=False
    )
```

time: 188 us -> 144 us (0.77)
  Pallas kernels: 186 us -> 142 us
    pallas_call x1, Pallas kernels: 186 us -> 142 us  [on_device(): pl.pallas_call(kernel, out_shape=pltpu.VMEM((ROWS, SCEN), jnp.float32), i...]
where the time goes in v3:
time: 144 us
  Pallas kernels  142 us (99%)
  local copies, waits for them, and re-layouts  2.02 us (1%)
    pallas_call x1, Pallas kernels, on_device(): pl.pallas_call(kernel, out_shape=pltpu.VMEM((ROWS, SCEN), jnp.float32), i...  142 us

profile of v3, /device:TPU:1, one launch (start us, length us, event | category | flops | bytes accessed | tf_op | source)
XLA Modules:
  0.0 144.4 jit_solution(1891031893243225)
XLA Ops:
  0.0 142.4 %substitute.1 = f32[1024,1024]{1,0:T(8,128)S(1)} custom-call(bf16[8,131072]{1,0:T(8,128)(2,1)} %rhs.1, bf16[1024,8192]{1,0:T(8,128)(2,1)} %panels.1), custom_call_target="tpu_custom_call" | custom-call | tf_op jit(solution)/shard_map/substitute/pallas_call | solution.py:491
  142.4 2.0 %copy.4 = f32[1024,1024]{1,0:T(8,128)} copy(f32[1024,1024]{1,0:T(8,128)S(1)} %substitute.1) | data formatting | bytes 8388608

commit v4 on v3

--- a/solution.py
+++ b/solution.py
@@ -50,7 +50,7 @@
 
 def kernel(rhs, panels, out, xs, acc, fac, rt, staged, passing, feeding, own_sem, fac_sem, send_sem, near_sem, last_sem,
            far_sem, swap_sem, rt_send, rt_recv, sc_send, pass_recv, pass_send,
-           feed_recv, feed_send):
+           feed_recv, feed_send, known):
     row, col = lax.axis_index("row"), lax.axis_index("col")
     me = row * 16 + col
     core = row % 2
@@ -84,10 +84,9 @@
     def rt_wait():
         pltpu.make_async_copy(rt, rt, rt_recv).wait()
 
-    def feeds():
+    def feeds(b):
         for h in range(2):
-            dx = (at["x"] - 2 - h) % 4
-            yield h, {"x": dx, "y": at["y"], "z": at["z"]}
+            yield h, {"x": (at["x"] - 2 * b - h) % 4, "y": at["y"], "z": (at["z"] - b // 2) % 4}
 
     def away(offset):
         apart = [jnp.minimum(offset[a], 4 - offset[a]) for a in "xyz"]
@@ -96,26 +95,27 @@
     def listed(way):
         return [(dz, m, dx) for m in range(4) for dz, dx in RELAYS[way][m]]
 
-    def feed():
-        for h, offset in feeds():
+    def feed(b):
+        for h, offset in feeds(b):
             hops = away(offset)
 
-            @pl.when((hops < 2) & (me != 2 + h))
+            @pl.when((hops < 2) & (me != 2 * b + h))
             def _():
-                rt_copy(jnp.int32(2 + h)).start()
+                rt_copy(jnp.int32(2 * b + h)).start()
             for way in WAYS:
                 axis, by = way
-                relay = {"x": 2 + h, "y": 0, "z": 0}
+                relay = {"x": (2 * b + h) % 4, "y": 0, "z": b // 2}
                 relay[axis] = (relay[axis] + by) % 4
                 for i, (dz, dy, dx) in enumerate(listed(way)):
                     @pl.when((offset["x"] == dx) & (offset["y"] == dy) & (offset["z"] == dz))
                     def _():
                         pltpu.make_async_remote_copy(
-                            src_ref=rows_to(jnp.int32(2 + h)), dst_ref=feeding.at[i], send_sem=rt_send, recv_sem=feed_recv,
+                            src_ref=rows_to(jnp.int32(2 * b + h)), dst_ref=feeding.at[b - 1, i], send_sem=rt_send,
+                            recv_sem=feed_recv.at[b - 1],
                             device_id=device(relay, core), device_id_type=MESH).start()
 
-    def feed_roles():
-        for h, offset in feeds():
+    def feed_roles(b):
+        for h, offset in feeds(b):
             for axis, by in WAYS:
                 here = offset[axis] == by % 4
                 for other in "xyz":
@@ -123,23 +123,24 @@
                         here = here & (offset[other] == 0)
                 yield h, (axis, by), here
 
-    def feed_on():
-        for h, way, here in feed_roles():
+    def feed_on(b):
+        for h, way, here in feed_roles(b):
             @pl.when(here)
             def _():
                 held = listed(way)
-                got = feeding.at[0:len(held)]
-                pltpu.make_async_copy(got, got, feed_recv).wait()
+                got = feeding.at[b - 1, 0:len(held)]
+                pltpu.make_async_copy(got, got, feed_recv.at[b - 1]).wait()
                 for i, (dz, dy, dx) in enumerate(held):
                     pltpu.make_async_remote_copy(
-                        src_ref=feeding.at[i], dst_ref=rt.at[core, dy, dz, (2 + h + dx) % 4], send_sem=feed_send,
-                        recv_sem=rt_recv, device_id=(0, 2 + h), device_id_type=MESH).start()
-
-    def feed_done():
-        for h, way, here in feed_roles():
+                        src_ref=feeding.at[b - 1, i], dst_ref=rt.at[core, dy, (b // 2 + dz) % 4, (2 * b + h + dx) % 4],
+                        send_sem=feed_send,
+                        recv_sem=rt_recv, device_id=(0, 2 * b + h), device_id_type=MESH).start()
+
+    def feed_done(b):
+        for h, way, here in feed_roles(b):
             @pl.when(here)
             def _():
-                got = feeding.at[0:len(listed(way))]
+                got = feeding.at[b - 1, 0:len(listed(way))]
                 pltpu.make_async_copy(got, got, feed_send).wait()
 
     def load_factor(k):
@@ -286,19 +287,19 @@
     def hand_out(k, m):
         parity = me % 2
 
-        def send(dz, dx, target, place):
+        def send(dz, dx, target, place, way=None):
             pltpu.make_async_remote_copy(
                 src_ref=staged.at[m, (at["z"] + dz) % 4, (at["x"] + dx) % 4], dst_ref=target, send_sem=sc_send,
                 recv_sem=own_sem.at[k] if place is None else pass_recv.at[k - 1, m],
                 device_id=(m * 2 + parity, (at["z"] + dz) % 4 * 4 + (at["x"] + dx) % 4) if place is None
-                else device(place, parity), device_id_type=MESH).start()
+                else device(place, 1 if way == WAYS[0] else parity), device_id_type=MESH).start()
 
         most = max(len(RELAYS[way][m]) for way in WAYS)
         for i in range(most):
             for axis, by in WAYS:
                 if i < len(RELAYS[axis, by][m]):
                     dz, dx = RELAYS[axis, by][m][i]
-                    send(dz, dx, passing.at[k - 1, m, i], moved(axis, by))
+                    send(dz, dx, passing.at[k - 1, m, i], moved(axis, by), (axis, by))
         for dz in range(4):
             for dx in range(4):
                 hops = sum(min(v, 4 - v) for v in (dz, dx, m))
@@ -328,18 +329,18 @@
             hand_out(k, m)
 
     def roles(k):
-        dx = (at["x"] - (2 * k) % 4 - core) % 4
-        dz = (at["z"] - k // 2) % 4
-        offset = {"x": dx, "y": at["y"], "z": dz}
-        for axis, by in WAYS:
-            here = offset[axis] == by % 4
-            for other in "xyz":
-                if other != axis:
-                    here = here & (offset[other] == 0)
-            yield (axis, by), here
+        for way in WAYS:
+            axis, by = way
+            for h in (0, 1) if way == WAYS[0] else (core,):
+                offset = {"x": (at["x"] - (2 * k) % 4 - h) % 4, "y": at["y"], "z": (at["z"] - k // 2) % 4}
+                here = offset[axis] == by % 4
+                for other in "xyz":
+                    if other != axis:
+                        here = here & (offset[other] == 0)
+                yield way, h, here & (core == 1) if way == WAYS[0] else here
 
     def pass_on(k):
-        for (axis, by), here in roles(k):
+        for (axis, by), h, here in roles(k):
             @pl.when(here)
             def _():
                 for m in ORDER:
@@ -349,13 +350,13 @@
                     got = passing.at[k - 1, m, 0:len(held)]
                     pltpu.make_async_copy(got, got, pass_recv.at[k - 1, m]).wait()
                     for i, (dz, dx) in enumerate(held):
-                        z, x = (k // 2 + dz) % 4, ((2 * k) % 4 + core + dx) % 4
+                        z, x = (k // 2 + dz) % 4, ((2 * k) % 4 + h + dx) % 4
                         pltpu.make_async_remote_copy(
-                            src_ref=passing.at[k - 1, m, i], dst_ref=xs.at[k, core, m, z, x], send_sem=pass_send,
-                            recv_sem=own_sem.at[k], device_id=(m * 2 + core, z * 4 + x), device_id_type=MESH).start()
+                            src_ref=passing.at[k - 1, m, i], dst_ref=xs.at[k, h, m, z, x], send_sem=pass_send,
+                            recv_sem=own_sem.at[k], device_id=(m * 2 + h, z * 4 + x), device_id_type=MESH).start()
 
     def pass_done(k):
-        for way, here in roles(k):
+        for way, _, here in roles(k):
             @pl.when(here)
             def _():
                 for m in range(4):
@@ -380,7 +381,7 @@
     pl.semaphore_signal(barrier, inc=1, device_id=device(at, 1 - core), device_id_type=MESH)
 
     expected = 10
-    for h, offset in feeds():
+    for h, offset in feeds(1):
         hops = away(offset)
         expected = expected + ((hops > 1) | ((hops == 1) & (core == 1))).astype(jnp.int32)
 
@@ -388,7 +389,7 @@
         def _():
             for axis, by in WAYS:
                 pl.semaphore_signal(barrier, inc=1, device_id=device(moved(axis, by), 1), device_id_type=MESH)
-    for h, way, here in feed_roles():
+    for h, way, here in feed_roles(1):
         @pl.when(here)
         def _():
             for dz, dy, dx in listed(way):
@@ -400,19 +401,12 @@
         piece = xs.at[k, core, at["y"], at["z"], at["x"]]
         pltpu.make_async_copy(piece, piece, own_sem.at[k]).wait()
 
-    def to_owners(*owners):
-        for owner in owners:
-            @pl.when(me != owner)
-            def _():
-                rt_copy(jnp.int32(owner)).start()
-
     def batch(first, last):
         return lambda: rt_batch(first, last)
 
     def nothing():
         pass
 
-    own_piece(0)
     def load_wait():
         for load in loads:
             load.wait()
@@ -424,14 +418,32 @@
         load_wait()
         multiply(0, 1)
 
-    slots = [(1, 1, 1, 13), (13, 19, 25, 55), (55, 59, 63, 91), (91, 99, 107, 128)]
-
-    def after_first():
-        to_owners(4, 5, 6, 7)
+    slots = {0: (1, 1, 1, 27), 1: (27, 32, 37, 59), 2: (59, 64, 69, 91), 3: (91, 101, 111, 128)}
+
+    for by in (1, 2, 3):
+        pl.semaphore_signal(known.at[0], inc=1, device_id=device(moved("x", by), core), device_id_type=MESH)
+
+    def opening():
+        feed(1)
+        pl.semaphore_wait(known.at[0], 3)
+        for by in (1, 2, 3):
+            pl.semaphore_signal(known.at[1], inc=1, device_id=device(moved("y", by), core), device_id_type=MESH)
+
+    def all_known():
+        pl.semaphore_wait(known.at[1], 3)
+        pl.semaphore_signal(known.at[2], inc=1, device_id=device(at, 1 - core), device_id_type=MESH)
+        pl.semaphore_wait(known.at[2], 1)
+        feed(2)
+        feed(3)
+        rt_batch(slots[0][1], slots[0][2])
+
+    def feeding_on():
+        for b in (1, 2, 3):
+            feed_on(b)
         rt_batch(slots[0][2], slots[0][3])
 
-    gather(0, (feed, nothing, feed_on), first_half)
-    after_first()
+    own_piece(0)
+    gather(0, (opening, all_known, feeding_on), first_half)
     for k in (1, 2, 3):
         @pl.when(my_block == k)
         def _():
@@ -445,7 +457,11 @@
         pass_on(k)
         own_piece(k)
         cuts = slots[k]
-        gather(k, [batch(cuts[i], cuts[i + 1]) for i in range(3)], half_of(k))
+
+        def early():
+            rt_batch(cuts[0], cuts[1])
+
+        gather(k, (early, batch(cuts[1], cuts[2]), batch(cuts[2], cuts[3])), half_of(k))
 
     is_owner = me < 2 * STEPS
 
@@ -483,7 +499,8 @@
 
     for k in (1, 2, 3):
         pass_done(k)
-    feed_done()
+    for b in (1, 2, 3):
+        feed_done(b)
 
 
 def on_device(rhs_scen, factor_panels):
@@ -500,9 +517,10 @@
             pltpu.VMEM((2, 4, 4, 4, 8, ROWS), jnp.bfloat16),
             pltpu.VMEM((4, 4, 4, 2, 8, SCEN), jnp.bfloat16),
             pltpu.VMEM((STEPS - 1, 4, MOST, 2, 8, SCEN), jnp.bfloat16),
-            pltpu.VMEM((TOTAL, 8, ROWS), jnp.bfloat16),
+            pltpu.VMEM((STEPS - 1, TOTAL, 8, ROWS), jnp.bfloat16),
             dma((STEPS,)), dma((STEPS,)), dma, dma((2, 2, 3, 3)), dma((2, 4, 3, 2)), dma((2,)), dma((2,)),
-            dma, dma, dma, dma((STEPS - 1, 4)), dma, dma, dma,
+            dma, dma, dma, dma((STEPS - 1, 4)), dma, dma((STEPS - 1,)), dma,
+            pltpu.SemaphoreType.REGULAR((3,)),
         ],
         compiler_params=pltpu.CompilerParams(collective_id=0, has_side_effects=True, vmem_limit_bytes=52 * 1024 * 1024),
         name="substitute",

time: 144 us -> 142 us (0.986)
  Pallas kernels: 142 us -> 140 us
    pallas_call x1, Pallas kernels: 142 us -> 140 us  [on_device(): pl.pallas_call(kernel, out_shape=pltpu.VMEM((ROWS, SCEN), jnp.float32), i...]
where the time goes in v4:
time: 142 us
  Pallas kernels  140 us (99%)
  local copies, waits for them, and re-layouts  2.02 us (1%)
    pallas_call x1, Pallas kernels, on_device(): pl.pallas_call(kernel, out_shape=pltpu.VMEM((ROWS, SCEN), jnp.float32), i...  140 us

profile of v4, /device:TPU:1, one launch (start us, length us, event | category | flops | bytes accessed | tf_op | source)
XLA Modules:
  0.0 142.2 jit_solution(15347467630581857496)
XLA Ops:
  0.0 140.2 %substitute.1 = f32[1024,1024]{1,0:T(8,128)S(1)} custom-call(bf16[8,131072]{1,0:T(8,128)(2,1)} %rhs.1, bf16[1024,8192]{1,0:T(8,128)(2,1)} %panels.1), custom_call_target="tpu_custom_call" | custom-call | tf_op jit(solution)/shard_map/substitute/pallas_call | solution.py:508
  140.2 2.0 %copy.4 = f32[1024,1024]{1,0:T(8,128)} copy(f32[1024,1024]{1,0:T(8,128)S(1)} %substitute.1) | data formatting | bytes 8388608

commit v5 on v4

--- a/solution.py
+++ b/solution.py
@@ -73,7 +73,7 @@
 
     def rt_batch(first, last):
         def one(j, carry):
-            dst = (me + j) % 128
+            dst = (me + j * 35) % 128
 
             @pl.when((dst < 2) | (dst > 7))
             def _():
@@ -418,7 +418,7 @@
         load_wait()
         multiply(0, 1)
 
-    slots = {0: (1, 1, 1, 27), 1: (27, 32, 37, 59), 2: (59, 64, 69, 91), 3: (91, 101, 111, 128)}
+    slots = {0: (1, 1, 1, 31), 1: (31, 35, 39, 65), 2: (65, 69, 73, 99), 3: (99, 107, 115, 128)}
 
     for by in (1, 2, 3):
         pl.semaphore_signal(known.at[0], inc=1, device_id=device(moved("x", by), core), device_id_type=MESH)

time: 142 us -> 132 us (0.930)
  Pallas kernels: 140 us -> 129 us
    pallas_call x1, Pallas kernels: 140 us -> 129 us  [on_device(): pl.pallas_call(kernel, out_shape=pltpu.VMEM((ROWS, SCEN), jnp.float32), i...]
where the time goes in v5:
time: 132 us
  Pallas kernels  129 us (98%)
  local copies, waits for them, and re-layouts  2.02 us (2%)
    pallas_call x1, Pallas kernels, on_device(): pl.pallas_call(kernel, out_shape=pltpu.VMEM((ROWS, SCEN), jnp.float32), i...  129 us

profile of v5, /device:TPU:1, one launch (start us, length us, event | category | flops | bytes accessed | tf_op | source)
XLA Modules:
  0.0 131.5 jit_solution(10598820010256427426)
XLA Ops:
  0.0 129.5 %substitute.1 = f32[1024,1024]{1,0:T(8,128)S(1)} custom-call(bf16[8,131072]{1,0:T(8,128)(2,1)} %rhs.1, bf16[1024,8192]{1,0:T(8,128)(2,1)} %panels.1), custom_call_target="tpu_custom_call" | custom-call | tf_op jit(solution)/shard_map/substitute/pallas_call | solution.py:508
  129.5 2.0 %copy.4 = f32[1024,1024]{1,0:T(8,128)} copy(f32[1024,1024]{1,0:T(8,128)S(1)} %substitute.1) | data formatting | bytes 8388608
